TPU v7x, 32 devices: a whole 2x2x4 slice. The times are simulated.
32 devices in a mesh: groups: 2 (over y), blk: 4 (over z), red: 2 (over x), sub: 2 (over core).
Axes of the slice: x: 2, y: 2, z: 4, core: 2. Of those that a mesh axis runs over, the one named last changes fastest.
Arguments:
- activations: bfloat16 [2, 16, 128, 8192], P('red', ('groups', 'blk', 'sub')), parts along dimension 1, may hold values from -6 to 6
- out_grads: bfloat16 [2, 16, 128, 8192], P('red', ('groups', 'blk', 'sub')), parts along dimension 1, may hold values from -6 to 6
- lengths: int32 [2, 16], P('red', ('groups', 'blk', 'sub')), parts along dimension 1, may hold values from 32 to 128
- proj_in: bfloat16 [8192, 256], P(('blk', 'red', 'sub')), may hold values from -0.0625 to 0.0625
- proj_out: bfloat16 [8192, 256], P(('blk', 'red', 'sub')), may hold values from -0.0625 to 0.0625
- queries: bfloat16 [512, 256, 256], P(('groups', 'red'), ('blk', 'sub')), parts along dimension 0, may hold values from -6 to 6
Outputs:
- scores: float32 [512, 16], P(('groups', 'blk', 'sub'), 'red'), parts along dimension 0
There are 2 independent parts, one for each index of `groups`. A program takes and returns all parts, laid end to end along the dimension named above; an argument that names none is the same for every part. Nothing has to cross between parts.
All inputs are finite; a program needn't handle non-finite values.
Results may differ from a plain program's by a relative error of at most 0.0051.
Values may be sent and summed in bfloat16 or wider, within the bound.
No kernel may reach another device: no remote copies, remote signals or barrier semaphores. Data moves between devices by JAX's collectives and lax.ppermute only.
A program may use at most 128 MiB of HBM per device.

v0:
```python
import math
import jax
import jax.numpy as jnp
from jax import lax
from jax.sharding import PartitionSpec as P

BS = 512
NS_STEPS = 2
BLOCKS = 128
DAMPING = 0.1
HIGH = lax.Precision.HIGHEST


def whole_inverse(fisher):
    ident = jnp.eye(BS, dtype=jnp.float32)
    trace = jnp.sum(fisher * ident, axis=(1, 2))
    damping = DAMPING * trace / BS
    hessian = fisher + damping[:, None, None] * ident
    scale = lax.rsqrt(jnp.sum(hessian * hessian, axis=(1, 2)))[:, None, None]
    inverse = scale * (2.0 * ident - scale * hessian)
    for sweep in range(NS_STEPS):
        image = jnp.einsum("kab,kbc->kac", hessian, inverse, precision=HIGH)
        inverse = jnp.einsum("kab,kbc->kac", inverse, 2.0 * ident - image, precision=HIGH)
    return inverse


def on_device(activations, out_grads, lengths, proj_in, proj_out, queries):
    ex_dev = activations.shape[1]
    seq_len = activations.shape[2]
    model_width = activations.shape[3]
    rank_in = proj_in.shape[1]
    rank_out = proj_out.shape[1]
    positions = lax.broadcasted_iota(jnp.int32, (ex_dev, seq_len), 1)
    live_mask = positions < lengths
    tok_rows = activations.reshape(ex_dev * seq_len, model_width)
    masked = jnp.where(
        live_mask.reshape(ex_dev * seq_len, 1),
        out_grads.reshape(ex_dev * seq_len, model_width),
        jnp.zeros((), out_grads.dtype),
    )
    first_sum = jnp.dot(
        tok_rows,
        lax.all_gather(proj_in, ("blk", "red", "sub"), axis=0, tiled=True),
        preferred_element_type=jnp.float32,
    )
    second_sum = jnp.dot(
        masked,
        lax.all_gather(proj_out, ("blk", "red", "sub"), axis=0, tiled=True),
        preferred_element_type=jnp.float32,
    )
    in_side = first_sum
    out_side = second_sum
    in_side = in_side.astype(jnp.bfloat16).reshape(ex_dev, seq_len, rank_in)
    out_side = out_side.astype(jnp.bfloat16).reshape(ex_dev, seq_len, rank_out)
    projected = jnp.einsum(
        "elo,eli->eoi", out_side, in_side, preferred_element_type=jnp.float32
    ).astype(jnp.bfloat16)
    gathered_q = lax.all_gather(queries, "red", axis=0, tiled=True)
    regrouped = lax.all_to_all(projected, ("blk", "sub"), split_axis=1, concat_axis=0, tiled=True)
    held = regrouped.shape[0]
    coords = regrouped.reshape(held, -1, BS)
    total_ex = held * lax.axis_size("red")
    every_coord = lax.all_gather(coords, "red", axis=0, tiled=True)
    fisher = (
        jnp.einsum("ekc,ekd->kcd", every_coord, every_coord, preferred_element_type=jnp.float32)
        / total_ex
    )
    inverse = whole_inverse(fisher)
    query_coords = gathered_q.reshape(gathered_q.shape[0], -1, BS).astype(jnp.float32)
    weighted = jnp.einsum("kcd,qkd->kcq", inverse, query_coords, precision=HIGH)
    partial_scores = jnp.einsum("kcq,ekc->qe", weighted, coords.astype(jnp.float32), precision=HIGH)
    scores = lax.psum_scatter(partial_scores, ("blk", "sub"), scatter_dimension=0, tiled=True)
    return scores * (1.0 / math.sqrt(BLOCKS))


def solution(mesh):
    placed = (
        P("red", ("groups", "blk", "sub"), None, None),
        P("red", ("groups", "blk", "sub"), None, None),
        P("red", ("groups", "blk", "sub")),
        P(("blk", "red", "sub"), None),
        P(("blk", "red", "sub"), None),
        P(("groups", "red"), ("blk", "sub"), None),
    )
    return jax.shard_map(
        on_device,
        mesh=mesh,
        in_specs=placed,
        out_specs=P(("groups", "blk", "sub"), "red"),
        check_vma=False,
    )
```

profile of v0, /device:TPU:0, one launch (start us, length us, event | category | flops | bytes accessed | tf_op | source)
XLA Modules:
  0.0 409.2 jit_solution(16152823896009520722)
XLA Ops:
  6.5 0.0 copy-start
  6.5 0.0 all-gather.4.cloned.1.call-start
  6.5 0.7 all-gather.4.cloned.1.call-update
  7.3 0.0 all-gather.6.cloned.1.call-start
  7.3 0.7 all-gather.6.cloned.1.call-update
  8.0 0.0 all-gather.8.cloned.1.call-start
  8.1 0.7 all-gather.8.cloned.1.call-update
  9.4 0.1 fusion.21
  9.5 53.1 %all-gather.4.cloned.1.call-done = bf16[8192,256]{1,0:T(8,128)(2,1)} async-done(((bf16[512,256]{1,0:T(8,128)(2,1)}), bf16[8192,256]{1,0:T(8,128)(2,1)}) %all-gather.4.cloned.1.call-update) | async-done | bytes 4194320 | tf_op jit(solution)/shard_map/all_gather | solution.py:48
  62.6 3.6 fusion.15
  66.2 47.5 %all-gather.6.cloned.1.call-done = bf16[8192,256]{1,0:T(8,128)(2,1)} async-done(((bf16[512,256]{1,0:T(8,128)(2,1)}), bf16[8192,256]{1,0:T(8,128)(2,1)}) %all-gather.6.cloned.1.call-update) | async-done | bytes 4194320 | tf_op jit(solution)/shard_map/all_gather | solution.py:43
  113.7 0.0 copy-done
  113.7 3.1 fusion.14
  116.8 0.2 copy.24
  117.1 0.5 broadcast.40
  117.6 1.4 reduce.2
  119.0 0.7 reshape.60
  119.7 3.4 all-to-all-start
  123.1 0.0 reduce-scatter.4.cloned.1.call-start
  123.1 0.1 fusion.20
  123.2 0.1 fusion.19
  123.3 47.2 %all-gather.8.cloned.1.call-done = bf16[256,32,256]{2,1,0:T(8,128)(2,1)} async-done(((bf16[128,32,256]{2,1,0:T(8,128)(2,1)}), bf16[256,32,256]{2,1,0:T(8,128)(2,1)}) %all-gather.8.cloned.1.call-update) | async-done | bytes 4194320 | tf_op jit(solution)/shard_map/all_gather | solution.py:58
  170.6 7.5 %copy.15 = bf16[256,32,256]{0,2,1:T(8,128)(2,1)} copy(bf16[256,32,256]{2,1,0:T(8,128)(2,1)} %all-gather.8.cloned.1.call-done) | data formatting | bytes 8388608 | tf_op jit(solution)/shard_map/all_gather | solution.py:58
  178.1 0.0 all-to-all-done
  178.1 0.1 reshape.61
  178.2 0.7 bitcast_reduce_fusion
  179.0 0.1 copy.14
  179.1 5.7 %all_gather.14 = bf16[16,16,512]{2,0,1:T(8,128)(2,1)S(1)} all-gather(bf16[8,16,512]{2,0,1:T(8,128)(2,1)S(1)} %copy.14), channel_id=1, replica_groups=mesh['groups'=2,'blk'=4,'red'=2,'sub'=2] {'red'}, dimensions={0}, use_global_device_ids=true | all-gather | bytes 393216 | tf_op jit(solution)/shard_map/all_gather | solution.py:63
  184.8 8.2 %multiply_reduce_fusion.1 = (f32[16]{0:T(128)S(1)}, f32[16,512,512]{2,1,0:T(8,128)}) fusion(f32[512,512]{1,0:T(8,128)S(1)} %fusion.21, bf16[16,16,512]{2,0,1:T(8,128)(2,1)S(1)} %all_gather.14), kind=kOutput, calls=%fused_computation.8 | convolution fusion | flops 142606320 | bytes 18088000 | tf_op jit(solution)/shard_map/ekc,ekd->kcd/dot_general | solution.py:65
  193.1 8.7 %multiply_reduce_fusion = f32[16]{0:T(128)S(1)} fusion(f32[512,512]{1,0:T(8,128)S(1)} %fusion.20, f32[16]{0:T(128)S(1)} %broadcast_multiply_fusion.1, f32[16,512,512]{2,1,0:T(8,128)} %get-tuple-element.6), kind=kLoop, calls=%fused_computation.6 | loop fusion | flops 20971504 | bytes 17825920 | tf_op jit(solution)/shard_map/reduce_sum | solution.py:19
  201.8 40.7 %fusion.4 = f32[16,512,512]{2,1,0:T(8,128)} fusion(f32[512,512]{1,0:T(8,128)S(1)} %fusion.19, f32[16]{0:T(128)S(1)} %rsqrt.7, f32[16,512,512]{2,1,0:T(8,128)} %get-tuple-element.6, f32[512,512]{1,0:T(8,128)S(1)} %fusion.20, f32[16]{0:T(128)S(1)} %broadcast_multiply_fusion.1), kind=kOutput, calls=%fused_computation.5 | convolution fusion | flops 25807552512 | bytes 35651712 | tf_op jit(solution)/shard_map/kab,kbc->kac/dot_general | solution.py:22
  242.5 36.6 %fusion.2 = f32[16,512,512]{2,1,0:T(8,128)} fusion(f32[16,512,512]{2,1,0:T(8,128)} %fusion.4, f32[512,512]{1,0:T(8,128)S(1)} %fusion.19, f32[16]{0:T(128)S(1)} %rsqrt.7, f32[16,512,512]{2,1,0:T(8,128)} %get-tuple-element.6, f32[512,512]{1,0:T(8,128)S(1)} %fusion.20, f32[16]{0:T(128)S(1)} %broadcast_multiply_fusion.1), kind=kOutput, calls=%fused_computation.2 | convolution fusion | flops 25799163904 | bytes 52428928 | tf_op jit(solution)/shard_map/kab,kbc->kac/dot_general | solution.py:23
  279.1 0.0 copy-start.2
  279.1 36.8 %fusion.27 = f32[16,512,512]{2,1,0:T(8,128)} fusion(f32[16,512,512]{2,1,0:T(8,128)} %fusion.2, f32[16,512,512]{2,1,0:T(8,128)} %get-tuple-element.6, f32[512,512]{1,0:T(8,128)S(1)} %fusion.20, f32[16]{0:T(128)S(1)} %broadcast_multiply_fusion.1), kind=kOutput, calls=%fused_computation.34 | convolution fusion | flops 25782386688 | bytes 51380288 | tf_op jit(solution)/shard_map/kab,kbc->kac/dot_general | solution.py:22
  315.9 0.0 copy-done.2
  315.9 33.2 %fusion = f32[16,512,512]{2,1,0:T(8,128)} fusion(f32[16,512,512]{2,1,0:T(8,128)S(1)} %copy-done.2, f32[16,512,512]{2,1,0:T(8,128)} %fusion.27, f32[512,512]{1,0:T(8,128)S(1)} %fusion.19), kind=kOutput, calls=%fused_computation | convolution fusion | flops 25773998080 | bytes 51380224 | tf_op jit(solution)/shard_map/kab,kbc->kac/dot_general | solution.py:23
  349.1 0.0 copy-start.1
  349.1 13.6 %fusion.28 = f32[16,512,256]{2,1,0:T(8,128)S(1)} fusion(f32[16,512,512]{2,1,0:T(8,128)} %fusion, bf16[256,16,512]{0,2,1:T(8,128)(2,1)} %bitcast.36), kind=kOutput, calls=%fused_computation.37 | convolution fusion | flops 12884901888 | bytes 29360128 | tf_op jit(solution)/shard_map/kcd,qkd->kcq/dot_general | solution.py:70
  362.8 7.3 %convolution_bitcast_fusion = f32[256,8]{1,0:T(8,128)} fusion(f32[16,512,256]{2,1,0:T(8,128)S(1)} %fusion.28, bf16[8,16,512]{2,1,0:T(8,128)(2,1)S(1)} %reshape.54), kind=kOutput, calls=%fused_computation.20 | convolution fusion | flops 201326592 | bytes 8527872 | tf_op jit(solution)/shard_map/kcq,ekc->qe/dot_general | solution.py:71
  370.1 0.0 reduce-scatter.4.cloned.1.call-update
  370.1 30.7 %reduce-scatter.4.cloned.1.call-done = f32[32,8]{1,0:T(8,128)} async-done(((f32[256,8]{1,0:T(8,128)}), f32[32,8]{1,0:T(8,128)}) %reduce-scatter.4.cloned.1.call-update) | async-done | bytes 1040
  400.8 0.8 copy.20
  401.6 0.6 broadcast_multiply_fusion
  402.2 0.0 copy-done.1
  (4 shorter events, 0.1 us)
Async XLA Ops:
  6.5 107.2 %copy-start = (bf16[1,1,128,8192]{3,2,1,0:T(8,128)(2,1)S(1)}, bf16[1,1,128,8192]{3,2,1,0:T(8,128)(2,1)}, u32[]{:S(2)}) copy-start(bf16[1,1,128,8192]{3,2,1,0:T(8,128)(2,1)} %param.6) | copy-start | bytes 6291460
  6.5 56.1 %all-gather.4.cloned.1.call-start = ((), (), s32[]{:S(2)}) async-start(), calls=%async_computation.2 | async-start | bytes 4456448 | tf_op jit(solution)/shard_map/all_gather | solution.py:48
  7.3 106.5 %all-gather.6.cloned.1.call-start = ((), (), s32[]{:S(2)}) async-start(), calls=%async_computation.3 | async-start | bytes 4456448 | tf_op jit(solution)/shard_map/all_gather | solution.py:43
  8.0 162.6 %all-gather.8.cloned.1.call-start = ((), (), s32[]{:S(2)}) async-start(), calls=%async_computation.4 | async-start | bytes 6291456 | tf_op jit(solution)/shard_map/all_gather | solution.py:58
  119.7 58.4 %all-to-all-start = ((bf16[8,2,4096]{2,1,0:T(2,128)(2,1)}), bf16[8,2,4096]{2,1,0:T(2,128)(2,1)S(1)}, u32[]{:S(2)}, u32[]{:S(2)}) async-start(bf16[8,2,4096]{2,1,0:T(2,128)(2,1)} %reshape.60), calls=%async_computation | async-start | bytes 262144 | tf_op jit(solution)/shard_map/all_to_all | solution.py:59
  123.1 277.8 %reduce-scatter.4.cloned.1.call-start = ((), (), s32[]{:S(2)}) async-start(), calls=%async_computation.5 | async-start | bytes 147456
  279.1 36.8 %copy-start.2 = (f32[16,512,512]{2,1,0:T(8,128)S(1)}, f32[16,512,512]{2,1,0:T(8,128)}, u32[]{:S(2)}) copy-start(f32[16,512,512]{2,1,0:T(8,128)} %fusion.2) | copy-start | bytes 50331652
  349.1 53.1 %copy-start.1 = (bf16[1,1,128,8192]{3,2,1,0:T(8,128)(2,1)S(1)}, bf16[1,1,128,8192]{3,2,1,0:T(8,128)(2,1)}, u32[]{:S(2)}) copy-start(bf16[1,1,128,8192]{3,2,1,0:T(8,128)(2,1)} %param.6) | copy-start | bytes 6291460
Sparse Core Ops, SparseCore 0:
  9.5 53.0 all-gather.3
  64.8 48.8 all-gather.5
  115.3 55.2 all-gather.7
  370.2 30.5 reduce-scatter.3
where the time goes:
time: 417 us; the launch traced here: 409 us
  matrix products  183 us (44%)
  waiting for transfers between devices  181 us (43%)
  between operations  14.4 us (3%)
  other arithmetic  11.1 us (3%)
  local copies, waits for them, and re-layouts  10.7 us (3%)
  blocking collectives  5.74 us (1%)
    dot_general x2, matrix products, whole_inverse(): image = jnp.einsum('kab,kbc->kac', hessian, inverse, precision=HIGH)  77.5 us
    dot_general x2, matrix products, whole_inverse(): jnp.einsum('kab,kbc->kac', inverse, 2.0 * ident - image, precision=HIGH)  69.8 us
    all_gather x1, waiting for transfers between devices, on_device(): lax.all_gather(proj_out, ('blk', 'red', 'sub'), axis=0, tiled=True)  53.1 us
    all_gather x1, waiting for transfers between devices, on_device(): lax.all_gather(proj_in, ('blk', 'red', 'sub'), axis=0, tiled=True)  47.5 us
    all_gather x1, waiting for transfers between devices, on_device(): gathered_q = lax.all_gather(queries, 'red', axis=0, tiled=True)  47.2 us
    unnamed x5, waiting for transfers between devices  32.8 us
    dot_general x1, matrix products, on_device(): weighted = jnp.einsum('kcd,qkd->kcq', inverse, query_coords, precision=HIGH)  13.6 us
    reduce_sum x1, other arithmetic, whole_inverse(): scale = lax.rsqrt(jnp.sum(hessian * hessian, axis=(1, 2)))[:, None, None]  8.73 us
  transfers between devices with their start and end apart: 5, of which 4 were waited for; matrix products, arithmetic and copies ran while one was open for 4% of the time, Pallas kernels for 0%

commit v1 on v0

--- a/solution.py
+++ b/solution.py
@@ -9,6 +9,24 @@
 BLOCKS = 128
 DAMPING = 0.1
 HIGH = lax.Precision.HIGHEST
+
+
+def collect(value, axis, dim):
+    ways, here, turn = (lax.axis_size(axis), lax.axis_index(axis), value.shape[dim])
+    shape = [n * ways if d == dim else n for d, n in enumerate(value.shape)]
+    full = lax.dynamic_update_slice_in_dim(
+        jnp.zeros(shape, value.dtype), value, here * turn, axis=dim
+    )
+    going_up = going_down = value
+    for far in range(1, ways // 2 + 1):
+        going_up = lax.ppermute(going_up, axis, [(d, (d + 1) % ways) for d in range(ways)])
+        full = lax.dynamic_update_slice_in_dim(full, going_up, (here - far) % ways * turn, axis=dim)
+        if 2 * far < ways:
+            going_down = lax.ppermute(going_down, axis, [(d, (d - 1) % ways) for d in range(ways)])
+            full = lax.dynamic_update_slice_in_dim(
+                full, going_down, (here + far) % ways * turn, axis=dim
+            )
+    return full
 
 
 def whole_inverse(fisher):
@@ -39,9 +57,7 @@
         jnp.zeros((), out_grads.dtype),
     )
     first_sum = jnp.dot(
-        tok_rows,
-        lax.all_gather(proj_in, ("blk", "red", "sub"), axis=0, tiled=True),
-        preferred_element_type=jnp.float32,
+        tok_rows, collect(proj_in, ("blk", "red", "sub"), 0), preferred_element_type=jnp.float32
     )
     second_sum = jnp.dot(
         masked,

time: 417 us -> 381 us (0.914)
  waiting for transfers between devices: 181 us -> 91.9 us
  starting transfers between devices: 3.5 us -> 36.1 us
  local copies, waits for them, and re-layouts: 10.7 us -> 31.3 us
    all_gather x1, waiting for transfers between devices: 53.1 us -> 0.01 us  [on_device(): lax.all_gather(proj_out, ('blk', 'red', 'sub'), axis=0, tiled=True)]
    all_gather x1 -> x0, waiting for transfers between devices: 47.5 us -> none  [on_device(): lax.all_gather(proj_in, ('blk', 'red', 'sub'), axis=0, tiled=True)]
    ppermute x0 -> x15, starting transfers between devices: none -> 32.6 us  [the longest x7 31.9 us: collect(): lax.ppermute(going_down, axis, [(d, (d - 1) % ways) for d in range(ways)])]
    ppermute x0 -> x15, waiting for transfers between devices: none -> 28.6 us  [the longest x8 16.2 us: collect(): lax.ppermute(going_up, axis, [(d, (d + 1) % ways) for d in range(ways)])]
    dynamic_update_slice x0 -> x16, local copies, waits for them, and re-layouts: none -> 18.3 us  [the longest x8 8.65 us: collect(): lax.dynamic_update_slice_in_dim(full, going_up, (here - far) % ways * tur...]
    all_gather x1, waiting for transfers between devices: 47.2 us -> 31.1 us  [on_device(): gathered_q = lax.all_gather(queries, 'red', axis=0, tiled=True)]
    unnamed x5 -> x4, waiting for transfers between devices: 32.8 us -> 32.1 us
  transfers between devices with their start and end apart: 5 -> 19, of which waited for: 4 -> 11; matrix products, arithmetic and copies ran while one was open for 4% -> 10% of each run, Pallas kernels for 0% -> 0%
where the time goes in v1:
time: 381 us; the launch traced here: 375 us
  matrix products  184 us (48%)
  waiting for transfers between devices  91.9 us (24%)
  starting transfers between devices  36.1 us (9%)
  local copies, waits for them, and re-layouts  31.3 us (8%)
  between operations  14.4 us (4%)
  other arithmetic  11.1 us (3%)
  blocking collectives  6.26 us (2%)
    dot_general x2, matrix products, whole_inverse(): image = jnp.einsum('kab,kbc->kac', hessian, inverse, precision=HIGH)  77.3 us
    dot_general x2, matrix products, whole_inverse(): jnp.einsum('kab,kbc->kac', inverse, 2.0 * ident - image, precision=HIGH)  70 us
    unnamed x4, waiting for transfers between devices  32.1 us
    ppermute x7, starting transfers between devices, collect(): lax.ppermute(going_down, axis, [(d, (d - 1) % ways) for d in range(ways)])  31.9 us
    all_gather x1, waiting for transfers between devices, on_device(): gathered_q = lax.all_gather(queries, 'red', axis=0, tiled=True)  31.1 us
    ppermute x8, waiting for transfers between devices, collect(): lax.ppermute(going_up, axis, [(d, (d + 1) % ways) for d in range(ways)])  16.2 us
    dot_general x1, matrix products, on_device(): weighted = jnp.einsum('kcd,qkd->kcq', inverse, query_coords, precision=HIGH)  13.5 us
    ppermute x7, waiting for transfers between devices, collect(): lax.ppermute(going_down, axis, [(d, (d - 1) % ways) for d in range(ways)])  12.5 us
  transfers between devices with their start and end apart: 19, of which 11 were waited for; matrix products, arithmetic and copies ran while one was open for 10% of the time, Pallas kernels for 0%

profile of v1, /device:TPU:0, one launch (start us, length us, event | category | flops | bytes accessed | tf_op | source)
XLA Modules:
  0.0 374.9 jit_solution(14649565497856240253)
XLA Ops:
  8.6 5.0 %collective-permute-start.1 = (bf16[512,256]{1,0:T(8,128)(2,1)}, bf16[512,256]{1,0:T(8,128)(2,1)}, u32[]{:S(2)}, u32[]{:S(2)}) collective-permute-start(bf16[512,256]{1,0:T(8,128)(2,1)} %param.9), channel_id=1, source_target_pairs={{0,15},{1,0},{2,1},{3,2},{4,3},{5,4},{6,5},{7,6},{8,7},{9,8},{10,9... | collective-permute-start | bytes 786440 | tf_op jit(solution)/shard_map/ppermute | solution.py:25
  13.6 4.3 %collective-permute-done = bf16[512,256]{1,0:T(8,128)(2,1)S(1)} collective-permute-done((bf16[512,256]{1,0:T(8,128)(2,1)}, bf16[512,256]{1,0:T(8,128)(2,1)S(1)}, u32[]{:S(2)}, u32[]{:S(2)}) %collective-permute-start) | collective-permute-done | bytes 262176 | tf_op jit(solution)/shard_map/ppermute | solution.py:22
  17.9 4.5 %collective-permute-start.3 = (bf16[512,256]{1,0:T(8,128)(2,1)}, bf16[512,256]{1,0:T(8,128)(2,1)}, u32[]{:S(2)}, u32[]{:S(2)}) collective-permute-start(bf16[512,256]{1,0:T(8,128)(2,1)} %collective-permute-done.1), channel_id=1, source_target_pairs={{0,15},{1,0},{2,1},{3,2},{4,3},{5,4},{6,5},{7,6},{8,7},{9,8},{10,9... | collective-permute-start | bytes 786440 | tf_op jit(solution)/shard_map/ppermute | solution.py:25
  22.4 5.1 %collective-permute-done.2 = bf16[512,256]{1,0:T(8,128)(2,1)} collective-permute-done((bf16[512,256]{1,0:T(8,128)(2,1)S(1)}, bf16[512,256]{1,0:T(8,128)(2,1)}, u32[]{:S(2)}, u32[]{:S(2)}) %collective-permute-start.2) | collective-permute-done | bytes 262176 | tf_op jit(solution)/shard_map/ppermute | solution.py:22
  27.7 4.5 %collective-permute-start.5 = (bf16[512,256]{1,0:T(8,128)(2,1)}, bf16[512,256]{1,0:T(8,128)(2,1)}, u32[]{:S(2)}, u32[]{:S(2)}) collective-permute-start(bf16[512,256]{1,0:T(8,128)(2,1)} %collective-permute-done.3), channel_id=1, source_target_pairs={{0,15},{1,0},{2,1},{3,2},{4,3},{5,4},{6,5},{7,6},{8,7},{9,8},{10,9... | collective-permute-start | bytes 786440 | tf_op jit(solution)/shard_map/ppermute | solution.py:25
  32.1 2.2 broadcast_in_dim.24
  34.4 1.7 constant_dynamic-update-slice_fusion.15
  36.7 1.3 collective-permute-done.4
  38.3 1.7 constant_dynamic-update-slice_fusion.14
  40.0 4.2 %collective-permute-start.7 = (bf16[512,256]{1,0:T(8,128)(2,1)}, bf16[512,256]{1,0:T(8,128)(2,1)S(1)}, u32[]{:S(2)}, u32[]{:S(2)}) collective-permute-start(bf16[512,256]{1,0:T(8,128)(2,1)} %collective-permute-done.5), channel_id=1, source_target_pairs={{0,15},{1,0},{2,1},{3,2},{4,3},{5,4},{6,5},{7,6},{8,7},{9,8},{10,9... | collective-permute-start | bytes 786440 | tf_op jit(solution)/shard_map/ppermute | solution.py:25
  44.1 1.7 constant_dynamic-update-slice_fusion.13
  45.8 0.9 collective-permute-done.6
  46.7 1.7 constant_dynamic-update-slice_fusion.12
  48.4 1.7 constant_dynamic-update-slice_fusion.11
  50.1 3.9 %collective-permute-done.7 = bf16[512,256]{1,0:T(8,128)(2,1)S(1)} collective-permute-done((bf16[512,256]{1,0:T(8,128)(2,1)}, bf16[512,256]{1,0:T(8,128)(2,1)S(1)}, u32[]{:S(2)}, u32[]{:S(2)}) %collective-permute-start.7) | collective-permute-done | bytes 262176 | tf_op jit(solution)/shard_map/ppermute | solution.py:25
  54.0 4.5 %collective-permute-start.9 = (bf16[512,256]{1,0:T(8,128)(2,1)S(1)}, bf16[512,256]{1,0:T(8,128)(2,1)S(1)}, u32[]{:S(2)}, u32[]{:S(2)}) collective-permute-start(bf16[512,256]{1,0:T(8,128)(2,1)S(1)} %collective-permute-done.7), channel_id=1, source_target_pairs={{0,15},{1,0},{2,1},{3,2},{4,3},{5,4},{6,5},{7,6},{8,7},{9,8},{10,9... | collective-permute-start | bytes 786440 | tf_op jit(solution)/shard_map/ppermute | solution.py:25
  59.2 1.7 constant_dynamic-update-slice_fusion.9
  60.9 1.7 constant_dynamic-update-slice_fusion.8
  62.6 1.1 collective-permute-done.9
  63.6 4.6 %collective-permute-start.11 = (bf16[512,256]{1,0:T(8,128)(2,1)S(1)}, bf16[512,256]{1,0:T(8,128)(2,1)S(1)}, u32[]{:S(2)}, u32[]{:S(2)}) collective-permute-start(bf16[512,256]{1,0:T(8,128)(2,1)S(1)} %collective-permute-done.9), channel_id=1, source_target_pairs={{0,15},{1,0},{2,1},{3,2},{4,3},{5,4},{6,5},{7,6},{8,7},{9,8},{10,9... | collective-permute-start | bytes 786440 | tf_op jit(solution)/shard_map/ppermute | solution.py:25
  68.3 0.7 constant_dynamic-update-slice_fusion.7
  69.8 0.7 constant_dynamic-update-slice_fusion.5
  70.5 5.8 %collective-permute-done.11 = bf16[512,256]{1,0:T(8,128)(2,1)S(1)} collective-permute-done((bf16[512,256]{1,0:T(8,128)(2,1)S(1)}, bf16[512,256]{1,0:T(8,128)(2,1)S(1)}, u32[]{:S(2)}, u32[]{:S(2)}) %collective-permute-start.11) | collective-permute-done | bytes 262176 | tf_op jit(solution)/shard_map/ppermute | solution.py:25
  76.3 4.6 %collective-permute-start.13 = (bf16[512,256]{1,0:T(8,128)(2,1)S(1)}, bf16[512,256]{1,0:T(8,128)(2,1)S(1)}, u32[]{:S(2)}, u32[]{:S(2)}) collective-permute-start(bf16[512,256]{1,0:T(8,128)(2,1)S(1)} %collective-permute-done.11), channel_id=1, source_target_pairs={{0,15},{1,0},{2,1},{3,2},{4,3},{5,4},{6,5},{7,6},{8,7},{9,8},{10,9... | collective-permute-start | bytes 786440 | tf_op jit(solution)/shard_map/ppermute | solution.py:25
  81.7 0.7 constant_dynamic-update-slice_fusion.3
  82.4 0.7 constant_dynamic-update-slice_fusion.2
  83.1 1.7 collective-permute-done.13
  84.8 0.8 constant_dynamic-update-slice_fusion.1
  85.6 4.6 %collective-permute-done.14 = bf16[512,256]{1,0:T(8,128)(2,1)S(1)} collective-permute-done((bf16[512,256]{1,0:T(8,128)(2,1)S(1)}, bf16[512,256]{1,0:T(8,128)(2,1)S(1)}, u32[]{:S(2)}, u32[]{:S(2)}) %collective-permute-start.14) | collective-permute-done | bytes 262176 | tf_op jit(solution)/shard_map/ppermute | solution.py:22
  90.2 0.8 constant_dynamic-update-slice_fusion
  90.9 3.8 %fusion.15 = bf16[128,256]{1,0:T(8,128)(2,1)S(1)} fusion(bf16[8192,256]{1,0:T(8,128)(2,1)} %all-gather.3.cloned.1.call-done, bf16[1,1,128,8192]{3,2,1,0:T(8,128)(2,1)} %param.7, pred[128]{0:T(512)(128)(4,1)S(1)} %iota_compare_fusion.1), kind=kOutput, calls=%fused_computation.22 | convolution fusion | flops 537952256 | bytes 6357120 | tf_op jit(solution)/shard_map/dot_general | solution.py:62
  94.8 3.7 fusion.14
  99.1 1.4 reduce.2
  101.2 3.4 all-to-all-start
  104.9 31.1 %all-gather.5.cloned.1.call-done = bf16[256,32,256]{2,1,0:T(8,128)(2,1)} async-done(((bf16[128,32,256]{2,1,0:T(8,128)(2,1)}), bf16[256,32,256]{2,1,0:T(8,128)(2,1)}) %all-gather.5.cloned.1.call-update) | async-done | bytes 4194320 | tf_op jit(solution)/shard_map/all_gather | solution.py:74
  136.1 7.5 %copy.15 = bf16[256,32,256]{0,2,1:T(8,128)(2,1)} copy(bf16[256,32,256]{2,1,0:T(8,128)(2,1)} %all-gather.5.cloned.1.call-done) | data formatting | bytes 8388608 | tf_op jit(solution)/shard_map/all_gather | solution.py:74
  143.7 0.7 bitcast_reduce_fusion
  144.6 6.3 %all_gather.10 = bf16[16,16,512]{2,0,1:T(8,128)(2,1)S(1)} all-gather(bf16[8,16,512]{2,0,1:T(8,128)(2,1)S(1)} %copy.14), channel_id=1, replica_groups=mesh['groups'=2,'blk'=4,'red'=2,'sub'=2] {'red'}, dimensions={0}, use_global_device_ids=true | all-gather | bytes 393216 | tf_op jit(solution)/shard_map/all_gather | solution.py:79
  150.9 8.2 %multiply_reduce_fusion.1 = (f32[16]{0:T(128)S(1)}, f32[16,512,512]{2,1,0:T(8,128)}) fusion(f32[512,512]{1,0:T(8,128)S(1)} %fusion.21, bf16[16,16,512]{2,0,1:T(8,128)(2,1)S(1)} %all_gather.10), kind=kOutput, calls=%fused_computation.8 | convolution fusion | flops 142606320 | bytes 18088000 | tf_op jit(solution)/shard_map/ekc,ekd->kcd/dot_general | solution.py:81
  159.1 8.7 %multiply_reduce_fusion = f32[16]{0:T(128)S(1)} fusion(f32[512,512]{1,0:T(8,128)S(1)} %fusion.20, f32[16]{0:T(128)S(1)} %broadcast_multiply_fusion.1, f32[16,512,512]{2,1,0:T(8,128)} %get-tuple-element.6), kind=kLoop, calls=%fused_computation.6 | loop fusion | flops 20971504 | bytes 17825920 | tf_op jit(solution)/shard_map/reduce_sum | solution.py:37
  167.9 40.4 %fusion.4 = f32[16,512,512]{2,1,0:T(8,128)} fusion(f32[512,512]{1,0:T(8,128)S(1)} %fusion.19, f32[16]{0:T(128)S(1)} %rsqrt.7, f32[16,512,512]{2,1,0:T(8,128)} %get-tuple-element.6, f32[512,512]{1,0:T(8,128)S(1)} %fusion.20, f32[16]{0:T(128)S(1)} %broadcast_multiply_fusion.1), kind=kOutput, calls=%fused_computation.5 | convolution fusion | flops 25807552512 | bytes 35651712 | tf_op jit(solution)/shard_map/kab,kbc->kac/dot_general | solution.py:40
  208.3 36.6 %fusion.2 = f32[16,512,512]{2,1,0:T(8,128)} fusion(f32[16,512,512]{2,1,0:T(8,128)} %fusion.4, f32[512,512]{1,0:T(8,128)S(1)} %fusion.19, f32[16]{0:T(128)S(1)} %rsqrt.7, f32[16,512,512]{2,1,0:T(8,128)} %get-tuple-element.6, f32[512,512]{1,0:T(8,128)S(1)} %fusion.20, f32[16]{0:T(128)S(1)} %broadcast_multiply_fusion.1), kind=kOutput, calls=%fused_computation.2 | convolution fusion | flops 25799163904 | bytes 52428928 | tf_op jit(solution)/shard_map/kab,kbc->kac/dot_general | solution.py:41
  244.9 36.9 %fusion.27 = f32[16,512,512]{2,1,0:T(8,128)} fusion(f32[16,512,512]{2,1,0:T(8,128)} %fusion.2, f32[16,512,512]{2,1,0:T(8,128)} %get-tuple-element.6, f32[512,512]{1,0:T(8,128)S(1)} %fusion.20, f32[16]{0:T(128)S(1)} %broadcast_multiply_fusion.1), kind=kOutput, calls=%fused_computation.50 | convolution fusion | flops 25782386688 | bytes 51380288 | tf_op jit(solution)/shard_map/kab,kbc->kac/dot_general | solution.py:40
  281.8 33.4 %fusion = f32[16,512,512]{2,1,0:T(8,128)} fusion(f32[16,512,512]{2,1,0:T(8,128)S(1)} %copy-done.2, f32[16,512,512]{2,1,0:T(8,128)} %fusion.27, f32[512,512]{1,0:T(8,128)S(1)} %fusion.19), kind=kOutput, calls=%fused_computation | convolution fusion | flops 25773998080 | bytes 51380224 | tf_op jit(solution)/shard_map/kab,kbc->kac/dot_general | solution.py:41
  315.2 13.5 %fusion.28 = f32[16,512,256]{2,1,0:T(8,128)S(1)} fusion(f32[16,512,512]{2,1,0:T(8,128)} %fusion, bf16[256,16,512]{0,2,1:T(8,128)(2,1)} %bitcast.36), kind=kOutput, calls=%fused_computation.53 | convolution fusion | flops 12884901888 | bytes 29360128 | tf_op jit(solution)/shard_map/kcd,qkd->kcq/dot_general | solution.py:86
  328.7 7.3 %convolution_bitcast_fusion = f32[256,8]{1,0:T(8,128)} fusion(f32[16,512,256]{2,1,0:T(8,128)S(1)} %fusion.28, bf16[8,16,512]{2,1,0:T(8,128)(2,1)S(1)} %reshape.54), kind=kOutput, calls=%fused_computation.20 | convolution fusion | flops 201326592 | bytes 8527872 | tf_op jit(solution)/shard_map/kcq,ekc->qe/dot_general | solution.py:87
  336.1 30.7 %reduce-scatter.4.cloned.1.call-done = f32[32,8]{1,0:T(8,128)} async-done(((f32[256,8]{1,0:T(8,128)}), f32[32,8]{1,0:T(8,128)}) %reduce-scatter.4.cloned.1.call-update) | async-done | bytes 1040
  366.8 0.8 copy.20
  (46 shorter events, 7.0 us)
Async XLA Ops:
  6.5 88.2 %copy-start = (bf16[1,1,128,8192]{3,2,1,0:T(8,128)(2,1)S(1)}, bf16[1,1,128,8192]{3,2,1,0:T(8,128)(2,1)}, u32[]{:S(2)}) copy-start(bf16[1,1,128,8192]{3,2,1,0:T(8,128)(2,1)} %param.6) | copy-start | bytes 6291460
  6.5 84.4 %all-gather.3.cloned.1.call-start = ((), (), s32[]{:S(2)}) async-start(), calls=%async_computation.2 | async-start | bytes 4456448 | tf_op jit(solution)/shard_map/all_gather | solution.py:64
  7.3 128.8 %all-gather.5.cloned.1.call-start = ((), (), s32[]{:S(2)}) async-start(), calls=%async_computation.3 | async-start | bytes 6291456 | tf_op jit(solution)/shard_map/all_gather | solution.py:74
  8.0 9.9 %collective-permute-start = (bf16[512,256]{1,0:T(8,128)(2,1)}, bf16[512,256]{1,0:T(8,128)(2,1)S(1)}, u32[]{:S(2)}, u32[]{:S(2)}) collective-permute-start(bf16[512,256]{1,0:T(8,128)(2,1)} %param.9), channel_id=1, source_target_pairs={{0,1},{1,2},{2,3},{3,4},{4,5},{5,6},{6,7},{7,8},{8,9},{9,10},{10,1... | collective-permute-start | bytes 786440 | tf_op jit(solution)/shard_map/ppermute | solution.py:22
  8.6 9.3 %collective-permute-start.1 = (bf16[512,256]{1,0:T(8,128)(2,1)}, bf16[512,256]{1,0:T(8,128)(2,1)}, u32[]{:S(2)}, u32[]{:S(2)}) collective-permute-start(bf16[512,256]{1,0:T(8,128)(2,1)} %param.9), channel_id=1, source_target_pairs={{0,15},{1,0},{2,1},{3,2},{4,3},{5,4},{6,5},{7,6},{8,7},{9,8},{10,9... | collective-permute-start | bytes 786440 | tf_op jit(solution)/shard_map/ppermute | solution.py:25
  17.9 4.5 %copy-start.3 = (bf16[512,256]{1,0:T(8,128)(2,1)}, bf16[512,256]{1,0:T(8,128)(2,1)S(1)}, u32[]{:S(2)}) copy-start(bf16[512,256]{1,0:T(8,128)(2,1)S(1)} %collective-permute-done) | copy-start | bytes 786436
  17.9 9.6 %collective-permute-start.2 = (bf16[512,256]{1,0:T(8,128)(2,1)S(1)}, bf16[512,256]{1,0:T(8,128)(2,1)}, u32[]{:S(2)}, u32[]{:S(2)}) collective-permute-start(bf16[512,256]{1,0:T(8,128)(2,1)S(1)} %collective-permute-done), channel_id=1, source_target_pairs={{0,1},{1,2},{2,3},{3,4},{4,5},{5,6},{6,7},{7,8},{8,9},{9,10},{10,1... | collective-permute-start | bytes 786440 | tf_op jit(solution)/shard_map/ppermute | solution.py:22
  17.9 9.8 %collective-permute-start.3 = (bf16[512,256]{1,0:T(8,128)(2,1)}, bf16[512,256]{1,0:T(8,128)(2,1)}, u32[]{:S(2)}, u32[]{:S(2)}) collective-permute-start(bf16[512,256]{1,0:T(8,128)(2,1)} %collective-permute-done.1), channel_id=1, source_target_pairs={{0,15},{1,0},{2,1},{3,2},{4,3},{5,4},{6,5},{7,6},{8,7},{9,8},{10,9... | collective-permute-start | bytes 786440 | tf_op jit(solution)/shard_map/ppermute | solution.py:25
  27.5 10.5 %collective-permute-start.4 = (bf16[512,256]{1,0:T(8,128)(2,1)}, bf16[512,256]{1,0:T(8,128)(2,1)S(1)}, u32[]{:S(2)}, u32[]{:S(2)}) collective-permute-start(bf16[512,256]{1,0:T(8,128)(2,1)} %collective-permute-done.2), channel_id=1, source_target_pairs={{0,1},{1,2},{2,3},{3,4},{4,5},{5,6},{6,7},{7,8},{8,9},{9,10},{10,1... | collective-permute-start | bytes 786440 | tf_op jit(solution)/shard_map/ppermute | solution.py:22
  27.7 12.3 %collective-permute-start.5 = (bf16[512,256]{1,0:T(8,128)(2,1)}, bf16[512,256]{1,0:T(8,128)(2,1)}, u32[]{:S(2)}, u32[]{:S(2)}) collective-permute-start(bf16[512,256]{1,0:T(8,128)(2,1)} %collective-permute-done.3), channel_id=1, source_target_pairs={{0,15},{1,0},{2,1},{3,2},{4,3},{5,4},{6,5},{7,6},{8,7},{9,8},{10,9... | collective-permute-start | bytes 786440 | tf_op jit(solution)/shard_map/ppermute | solution.py:25
  38.0 8.7 %collective-permute-start.6 = (bf16[512,256]{1,0:T(8,128)(2,1)S(1)}, bf16[512,256]{1,0:T(8,128)(2,1)}, u32[]{:S(2)}, u32[]{:S(2)}) collective-permute-start(bf16[512,256]{1,0:T(8,128)(2,1)S(1)} %collective-permute-done.4), channel_id=1, source_target_pairs={{0,1},{1,2},{2,3},{3,4},{4,5},{5,6},{6,7},{7,8},{8,9},{9,10},{10,1... | collective-permute-start | bytes 786440 | tf_op jit(solution)/shard_map/ppermute | solution.py:22
  40.0 14.0 %collective-permute-start.7 = (bf16[512,256]{1,0:T(8,128)(2,1)}, bf16[512,256]{1,0:T(8,128)(2,1)S(1)}, u32[]{:S(2)}, u32[]{:S(2)}) collective-permute-start(bf16[512,256]{1,0:T(8,128)(2,1)} %collective-permute-done.5), channel_id=1, source_target_pairs={{0,15},{1,0},{2,1},{3,2},{4,3},{5,4},{6,5},{7,6},{8,7},{9,8},{10,9... | collective-permute-start | bytes 786440 | tf_op jit(solution)/shard_map/ppermute | solution.py:25
  46.7 12.5 %collective-permute-start.8 = (bf16[512,256]{1,0:T(8,128)(2,1)}, bf16[512,256]{1,0:T(8,128)(2,1)S(1)}, u32[]{:S(2)}, u32[]{:S(2)}) collective-permute-start(bf16[512,256]{1,0:T(8,128)(2,1)} %collective-permute-done.6), channel_id=1, source_target_pairs={{0,1},{1,2},{2,3},{3,4},{4,5},{5,6},{6,7},{7,8},{8,9},{9,10},{10,1... | collective-permute-start | bytes 786440 | tf_op jit(solution)/shard_map/ppermute | solution.py:22
  54.0 9.6 %collective-permute-start.9 = (bf16[512,256]{1,0:T(8,128)(2,1)S(1)}, bf16[512,256]{1,0:T(8,128)(2,1)S(1)}, u32[]{:S(2)}, u32[]{:S(2)}) collective-permute-start(bf16[512,256]{1,0:T(8,128)(2,1)S(1)} %collective-permute-done.7), channel_id=1, source_target_pairs={{0,15},{1,0},{2,1},{3,2},{4,3},{5,4},{6,5},{7,6},{8,7},{9,8},{10,9... | collective-permute-start | bytes 786440 | tf_op jit(solution)/shard_map/ppermute | solution.py:25
  59.2 9.8 %collective-permute-start.10 = (bf16[512,256]{1,0:T(8,128)(2,1)S(1)}, bf16[512,256]{1,0:T(8,128)(2,1)S(1)}, u32[]{:S(2)}, u32[]{:S(2)}) collective-permute-start(bf16[512,256]{1,0:T(8,128)(2,1)S(1)} %collective-permute-done.8), channel_id=1, source_target_pairs={{0,1},{1,2},{2,3},{3,4},{4,5},{5,6},{6,7},{7,8},{8,9},{9,10},{10,1... | collective-permute-start | bytes 786440 | tf_op jit(solution)/shard_map/ppermute | solution.py:22
  63.6 12.7 %collective-permute-start.11 = (bf16[512,256]{1,0:T(8,128)(2,1)S(1)}, bf16[512,256]{1,0:T(8,128)(2,1)S(1)}, u32[]{:S(2)}, u32[]{:S(2)}) collective-permute-start(bf16[512,256]{1,0:T(8,128)(2,1)S(1)} %collective-permute-done.9), channel_id=1, source_target_pairs={{0,15},{1,0},{2,1},{3,2},{4,3},{5,4},{6,5},{7,6},{8,7},{9,8},{10,9... | collective-permute-start | bytes 786440 | tf_op jit(solution)/shard_map/ppermute | solution.py:25
  69.0 12.7 %collective-permute-start.12 = (bf16[512,256]{1,0:T(8,128)(2,1)S(1)}, bf16[512,256]{1,0:T(8,128)(2,1)S(1)}, u32[]{:S(2)}, u32[]{:S(2)}) collective-permute-start(bf16[512,256]{1,0:T(8,128)(2,1)S(1)} %collective-permute-done.10), channel_id=1, source_target_pairs={{0,1},{1,2},{2,3},{3,4},{4,5},{5,6},{6,7},{7,8},{8,9},{9,10},{10,1... | collective-permute-start | bytes 786440 | tf_op jit(solution)/shard_map/ppermute | solution.py:22
  76.3 8.5 %collective-permute-start.13 = (bf16[512,256]{1,0:T(8,128)(2,1)S(1)}, bf16[512,256]{1,0:T(8,128)(2,1)S(1)}, u32[]{:S(2)}, u32[]{:S(2)}) collective-permute-start(bf16[512,256]{1,0:T(8,128)(2,1)S(1)} %collective-permute-done.11), channel_id=1, source_target_pairs={{0,15},{1,0},{2,1},{3,2},{4,3},{5,4},{6,5},{7,6},{8,7},{9,8},{10,9... | collective-permute-start | bytes 786440 | tf_op jit(solution)/shard_map/ppermute | solution.py:25
  81.7 8.5 %collective-permute-start.14 = (bf16[512,256]{1,0:T(8,128)(2,1)S(1)}, bf16[512,256]{1,0:T(8,128)(2,1)S(1)}, u32[]{:S(2)}, u32[]{:S(2)}) collective-permute-start(bf16[512,256]{1,0:T(8,128)(2,1)S(1)} %collective-permute-done.12), channel_id=1, source_target_pairs={{0,1},{1,2},{2,3},{3,4},{4,5},{5,6},{6,7},{7,8},{8,9},{9,10},{10,1... | collective-permute-start | bytes 786440 | tf_op jit(solution)/shard_map/ppermute | solution.py:22
  101.2 42.3 %all-to-all-start = ((bf16[8,2,4096]{2,1,0:T(2,128)(2,1)}), bf16[8,2,4096]{2,1,0:T(2,128)(2,1)S(1)}, u32[]{:S(2)}, u32[]{:S(2)}) async-start(bf16[8,2,4096]{2,1,0:T(2,128)(2,1)} %reshape.60), calls=%async_computation | async-start | bytes 262144 | tf_op jit(solution)/shard_map/all_to_all | solution.py:75
  104.6 262.1 %reduce-scatter.4.cloned.1.call-start = ((), (), s32[]{:S(2)}) async-start(), calls=%async_computation.4 | async-start | bytes 147456
  244.9 36.9 %copy-start.2 = (f32[16,512,512]{2,1,0:T(8,128)S(1)}, f32[16,512,512]{2,1,0:T(8,128)}, u32[]{:S(2)}) copy-start(f32[16,512,512]{2,1,0:T(8,128)} %fusion.2) | copy-start | bytes 50331652
  315.2 52.9 %copy-start.1 = (bf16[1,1,128,8192]{3,2,1,0:T(8,128)(2,1)S(1)}, bf16[1,1,128,8192]{3,2,1,0:T(8,128)(2,1)}, u32[]{:S(2)}) copy-start(bf16[1,1,128,8192]{3,2,1,0:T(8,128)(2,1)} %param.6) | copy-start | bytes 6291460
Sparse Core Ops, SparseCore 0:
  9.5 67.5 all-gather.2
  78.6 57.4 all-gather.4
  336.2 30.4 reduce-scatter.3
